TPU v7x, 32 devices: a whole 2x2x4 slice. The times are simulated.
32 devices in a mesh: fsdp: 8 (over z, x), rep: 4 (over y, core).
Axes of the slice: x: 2, y: 2, z: 4, core: 2. Of those that a mesh axis runs over, the one named last changes fastest.
Arguments:
- latents: float32 [256, 256, 384], P(('fsdp', 'rep')), may hold values from -6 to 6
- condition: float32 [256, 384], P(('fsdp', 'rep')), may hold values from -6 to 6
- cotangent: float32 [256, 256, 384], P(('fsdp', 'rep')), may hold values from -6 to 6
- w_ada: bfloat16 [2, 384, 2304], P(None, 'fsdp'), may hold values from -0.3125 to 0.3125
- b_ada: bfloat16 [2, 2304], P(None, 'fsdp'), may hold values from -3 to 3
- w_qkv: bfloat16 [2, 384, 1152], P(None, 'fsdp'), may hold values from -0.3125 to 0.3125
- qv_bias: bfloat16 [2, 768], P(None, 'fsdp'), may hold values from -3 to 3
- w_out: bfloat16 [2, 384, 384], P(None, 'fsdp'), may hold values from -1.25 to 1.25
- b_out: bfloat16 [2, 384], P(None, 'fsdp'), may hold values from -3 to 3
- w_up: bfloat16 [2, 384, 1536], P(None, 'fsdp'), may hold values from -0.3125 to 0.3125
- b_up: bfloat16 [2, 1536], P(None, 'fsdp'), may hold values from -3 to 3
- w_down: bfloat16 [2, 1536, 384], P(None, 'fsdp'), may hold values from -0.15625 to 0.15625
- b_down: bfloat16 [2, 384], P(None, 'fsdp'), may hold values from -3 to 3
Outputs:
- output: float32 [256, 256, 384], P(('fsdp', 'rep'))
- grad_latents: float32 [256, 256, 384], P(('fsdp', 'rep'))
- grad_condition: float32 [256, 384], P(('fsdp', 'rep'))
- grad_w_ada: float32 [2, 384, 2304], P(None, 'fsdp')
- grad_b_ada: float32 [2, 2304], P(None, 'fsdp')
- grad_w_qkv: float32 [2, 384, 1152], P(None, 'fsdp')
- grad_qv_bias: float32 [2, 768], P(None, 'fsdp')
- grad_w_out: float32 [2, 384, 384], P(None, 'fsdp')
- grad_b_out: float32 [2, 384], P(None, 'fsdp')
- grad_w_up: float32 [2, 384, 1536], P(None, 'fsdp')
- grad_b_up: float32 [2, 1536], P(None, 'fsdp')
- grad_w_down: float32 [2, 1536, 384], P(None, 'fsdp')
- grad_b_down: float32 [2, 384], P(None, 'fsdp')
All inputs are finite; a program needn't handle non-finite values.
Results may differ from a plain program's by a relative error of at most 0.029.
The roundings to bfloat16 on the way count: a program that leaves them out, or rounds other values in their place, can miss the bound.
Values may be sent and summed in bfloat16 or wider, within the bound.
No kernel may reach another device: no remote copies, remote signals or barrier semaphores. Data moves between devices by JAX's collectives and lax.ppermute only.
A program may use at most 320 MiB of HBM per device.

v0:
```python
import jax
import jax.numpy as jnp
from jax import lax
from jax.sharding import PartitionSpec as P

LAYERS = 2
GELU_C = 0.7978845608028654
GELU_A = 0.044715
EPS = 1e-06


def as_sent(shard):

    def short(part):
        return part.astype(jnp.bfloat16) if part.dtype == jnp.float32 else part

    return jax.tree.map(short, shard)


def pair_product(form, left, right):
    return jnp.einsum(form, left, right, preferred_element_type=jnp.float32)


def matmul(inputs, weight):
    flattened = inputs.reshape(-1, inputs.shape[-1])
    result = jnp.dot(flattened, weight, preferred_element_type=jnp.float32)
    return result.reshape(inputs.shape[:-1] + (weight.shape[-1],))


def matmul_back(grads, weight):
    flattened = grads.reshape(-1, grads.shape[-1])
    result = lax.dot_general(
        flattened, weight, (((1,), (1,)), ((), ())), preferred_element_type=jnp.float32
    )
    return result.reshape(grads.shape[:-1] + (weight.shape[0],))


def outer_sum(left, right):
    return lax.dot_general(
        left.reshape(-1, left.shape[-1]),
        right.reshape(-1, right.shape[-1]),
        (((0,), (0,)), ((), ())),
        preferred_element_type=jnp.float32,
    )


def norm_rows(stream):
    centered = stream - jnp.mean(stream, axis=-1, keepdims=True)
    inverse = lax.rsqrt(jnp.mean(centered * centered, axis=-1, keepdims=True) + EPS)
    return (centered * inverse, inverse)


def norm_back(grad_normed, normed, inverse):
    return inverse * (
        grad_normed
        - jnp.mean(grad_normed, axis=-1, keepdims=True)
        - normed * jnp.mean(grad_normed * normed, axis=-1, keepdims=True)
    )


def gelu_parts(pre_act):
    tanh_part = jnp.tanh(GELU_C * (pre_act + GELU_A * pre_act * pre_act * pre_act))
    value_part = 0.5 * pre_act * (1.0 + tanh_part)
    slope_part = 0.5 * (1.0 + tanh_part) + 0.5 * pre_act * (
        1.0 - tanh_part * tanh_part
    ) * GELU_C * (1.0 + 3.0 * GELU_A * pre_act * pre_act)
    return (value_part, slope_part)


def forward_pieces(stream, cond_rows, params):
    w_ada, b_ada, w_qkv, qv_bias, w_out, b_out, w_up, b_up, w_down, b_down = params
    model_width = stream.shape[-1]
    head_count = model_width // 64
    silu_cond = jax.nn.silu(cond_rows).astype(jnp.bfloat16)
    modulation = jnp.dot(silu_cond, w_ada, preferred_element_type=jnp.float32) + b_ada.astype(
        jnp.float32
    )
    pieces = [modulation[:, None, i * model_width : (i + 1) * model_width] for i in range(6)]
    shift1, scale1, gate1, shift2, scale2, gate2 = pieces
    normed1, inverse1 = norm_rows(stream)
    attn_in = (normed1 * (1.0 + scale1) + shift1).astype(jnp.bfloat16)
    bias_query = qv_bias[:model_width].astype(jnp.float32)
    bias_value = qv_bias[model_width:].astype(jnp.float32)
    full_bias = jnp.concatenate([bias_query, jnp.zeros_like(bias_query), bias_value])
    projected = (matmul(attn_in, w_qkv) + full_bias).astype(jnp.bfloat16)
    head_shape = stream.shape[:2] + (head_count, 64)
    query = projected[..., :model_width].reshape(head_shape)
    key_heads = projected[..., model_width : 2 * model_width].reshape(head_shape)
    value_heads = projected[..., 2 * model_width :].reshape(head_shape)
    scores = pair_product("bqhe,bkhe->bhqk", query, key_heads) * 0.125
    log_total = jax.nn.logsumexp(scores, axis=-1, keepdims=True)
    attention = jnp.exp(scores - log_total)
    attention_b = attention.astype(jnp.bfloat16)
    attended = (
        pair_product("bhqk,bkhe->bqhe", attention_b, value_heads)
        .astype(jnp.bfloat16)
        .reshape(stream.shape)
    )
    branch = matmul(attended, w_out) + b_out.astype(jnp.float32)
    middle = stream + gate1 * branch
    normed2, inverse2 = norm_rows(middle)
    mlp_in = (normed2 * (1.0 + scale2) + shift2).astype(jnp.bfloat16)
    hidden_pre = matmul(mlp_in, w_up) + b_up.astype(jnp.float32)
    activated_f, slope = gelu_parts(hidden_pre)
    activated = activated_f.astype(jnp.bfloat16)
    mlp_out = matmul(activated, w_down) + b_down.astype(jnp.float32)
    result = middle + gate2 * mlp_out
    saved = (
        silu_cond,
        pieces,
        normed1,
        inverse1,
        attn_in,
        query,
        key_heads,
        value_heads,
        attention,
        attention_b,
        attended,
        branch,
        normed2,
        inverse2,
        mlp_in,
        slope,
        activated,
        mlp_out,
    )
    return (result, saved)


def layer_forward(stream, cond_rows, params):
    return forward_pieces(stream, cond_rows, params)[0]


def layer_grads(stream, cond_rows, params, grad_result):
    w_ada, b_ada, w_qkv, qv_bias, w_out, b_out, w_up, b_up, w_down, b_down = params
    result, saved = forward_pieces(stream, cond_rows, params)
    (
        silu_cond,
        pieces,
        normed1,
        inverse1,
        attn_in,
        query,
        key_heads,
        value_heads,
        attention,
        attention_b,
        attended,
        branch,
        normed2,
        inverse2,
        mlp_in,
        slope,
        activated,
        mlp_out,
    ) = saved
    shift1, scale1, gate1, shift2, scale2, gate2 = pieces
    grad_z = gate2 * grad_result
    grad_z_b = grad_z.astype(jnp.bfloat16)
    grad_gate2 = jnp.sum(grad_result * mlp_out, axis=1)
    grad_b_down = jnp.sum(grad_z, axis=(0, 1))
    grad_w_down = outer_sum(activated, grad_z_b)
    grad_pre = matmul_back(grad_z_b, w_down) * slope
    grad_pre_b = grad_pre.astype(jnp.bfloat16)
    grad_b_up = jnp.sum(grad_pre, axis=(0, 1))
    grad_w_up = outer_sum(mlp_in, grad_pre_b)
    grad_mlp_in = matmul_back(grad_pre_b, w_up)
    grad_scale2 = jnp.sum(grad_mlp_in * normed2, axis=1)
    grad_shift2 = jnp.sum(grad_mlp_in, axis=1)
    grad_middle = grad_result + norm_back(grad_mlp_in * (1.0 + scale2), normed2, inverse2)
    grad_branch = gate1 * grad_middle
    grad_branch_b = grad_branch.astype(jnp.bfloat16)
    grad_gate1 = jnp.sum(grad_middle * branch, axis=1)
    grad_b_out = jnp.sum(grad_branch, axis=(0, 1))
    grad_w_out = outer_sum(attended, grad_branch_b)
    grad_attended = matmul_back(grad_branch_b, w_out).astype(jnp.bfloat16).reshape(query.shape)
    grad_value = pair_product("bhqk,bqhe->bkhe", attention_b, grad_attended)
    grad_probs = pair_product("bqhe,bkhe->bhqk", grad_attended, value_heads)
    row_dot = jnp.sum(attention * grad_probs, axis=-1, keepdims=True)
    grad_scores = (attention * (grad_probs - row_dot) * 0.125).astype(jnp.bfloat16)
    grad_query = pair_product("bhqk,bkhe->bqhe", grad_scores, key_heads)
    grad_key = pair_product("bhqk,bqhe->bkhe", grad_scores, query)
    flat_shape = stream.shape
    grad_proj = jnp.concatenate(
        [
            grad_query.reshape(flat_shape),
            grad_key.reshape(flat_shape),
            grad_value.reshape(flat_shape),
        ],
        axis=-1,
    )
    grad_proj_b = grad_proj.astype(jnp.bfloat16)
    grad_qv_bias = jnp.concatenate(
        [
            jnp.sum(grad_query.reshape(flat_shape), axis=(0, 1)),
            jnp.sum(grad_value.reshape(flat_shape), axis=(0, 1)),
        ]
    )
    grad_w_qkv = outer_sum(attn_in, grad_proj_b)
    grad_attn_in = matmul_back(grad_proj_b, w_qkv)
    grad_scale1 = jnp.sum(grad_attn_in * normed1, axis=1)
    grad_shift1 = jnp.sum(grad_attn_in, axis=1)
    grad_stream = grad_middle + norm_back(grad_attn_in * (1.0 + scale1), normed1, inverse1)
    grad_mod = jnp.concatenate(
        [grad_shift1, grad_scale1, grad_gate1, grad_shift2, grad_scale2, grad_gate2], axis=-1
    )
    grad_w_ada = jnp.dot(silu_cond.astype(jnp.float32).T, grad_mod, precision=lax.Precision.HIGHEST)
    grad_b_ada = jnp.sum(grad_mod, axis=0)
    grad_silu = jnp.dot(grad_mod, w_ada.astype(jnp.float32).T, precision=lax.Precision.HIGHEST)
    sigmoid_c = jax.nn.sigmoid(cond_rows)
    grad_cond = grad_silu * sigmoid_c * (1.0 + cond_rows * (1.0 - sigmoid_c))
    gradients = (
        grad_w_ada,
        grad_b_ada,
        grad_w_qkv,
        grad_qv_bias,
        grad_w_out,
        grad_b_out,
        grad_w_up,
        grad_b_up,
        grad_w_down,
        grad_b_down,
    )
    return (grad_stream, grad_cond, gradients)


def body(
    latents,
    condition,
    cotangent,
    w_ada,
    b_ada,
    w_qkv,
    qv_bias,
    w_out,
    b_out,
    w_up,
    b_up,
    w_down,
    b_down,
):
    stacked = (w_ada, b_ada, w_qkv, qv_bias, w_out, b_out, w_up, b_up, w_down, b_down)
    inputs = []
    kept_weights = []
    stream = latents
    for layer_index in range(LAYERS):
        owned_rows = tuple((weight[layer_index] for weight in stacked))
        params = jax.tree.map(
            lambda part, own: part.astype(own.dtype),
            lax.all_gather(as_sent(owned_rows), "fsdp", axis=0, tiled=True),
            owned_rows,
        )
        kept_weights.append(params)
        inputs.append(stream)
        stream = layer_forward(stream, condition, params)
    grad_stream = cotangent
    grad_cond = jnp.zeros(condition.shape, jnp.float32)
    shards = [None] * LAYERS
    for layer_index in reversed(range(LAYERS)):
        owned_rows = tuple((weight[layer_index] for weight in stacked))
        params = jax.tree.map(
            lambda part, own: part.astype(own.dtype),
            lax.all_gather(as_sent(owned_rows), "fsdp", axis=0, tiled=True),
            owned_rows,
        )
        grad_stream, cond_part, gradients = layer_grads(
            inputs[layer_index], condition, params, grad_stream
        )
        grad_cond = grad_cond + cond_part
        owned_sums = (
            lax.psum_scatter(
                gradients[0].astype(jnp.bfloat16), "fsdp", scatter_dimension=0, tiled=True
            ).astype(jnp.float32),
            lax.psum_scatter(
                gradients[1].astype(jnp.bfloat16), "fsdp", scatter_dimension=0, tiled=True
            ).astype(jnp.float32),
            lax.psum_scatter(
                gradients[2].astype(jnp.bfloat16), "fsdp", scatter_dimension=0, tiled=True
            ).astype(jnp.float32),
            lax.psum_scatter(
                gradients[3].astype(jnp.bfloat16), "fsdp", scatter_dimension=0, tiled=True
            ).astype(jnp.float32),
            lax.psum_scatter(
                gradients[4].astype(jnp.bfloat16), "fsdp", scatter_dimension=0, tiled=True
            ).astype(jnp.float32),
            lax.psum_scatter(
                gradients[5].astype(jnp.bfloat16), "fsdp", scatter_dimension=0, tiled=True
            ).astype(jnp.float32),
            lax.psum_scatter(
                gradients[6].astype(jnp.bfloat16), "fsdp", scatter_dimension=0, tiled=True
            ).astype(jnp.float32),
            lax.psum_scatter(
                gradients[7].astype(jnp.bfloat16), "fsdp", scatter_dimension=0, tiled=True
            ).astype(jnp.float32),
            lax.psum_scatter(
                gradients[8].astype(jnp.bfloat16), "fsdp", scatter_dimension=0, tiled=True
            ).astype(jnp.float32),
            lax.psum_scatter(
                gradients[9].astype(jnp.bfloat16), "fsdp", scatter_dimension=0, tiled=True
            ).astype(jnp.float32),
        )
        owned_sums = (
            lax.psum(owned_sums[0].astype(jnp.bfloat16), "rep").astype(jnp.float32),
            lax.psum(owned_sums[1].astype(jnp.bfloat16), "rep").astype(jnp.float32),
            lax.psum(owned_sums[2].astype(jnp.bfloat16), "rep").astype(jnp.float32),
            lax.psum(owned_sums[3].astype(jnp.bfloat16), "rep").astype(jnp.float32),
            lax.psum(owned_sums[4].astype(jnp.bfloat16), "rep").astype(jnp.float32),
            lax.psum(owned_sums[5].astype(jnp.bfloat16), "rep").astype(jnp.float32),
            lax.psum(owned_sums[6].astype(jnp.bfloat16), "rep").astype(jnp.float32),
            lax.psum(owned_sums[7].astype(jnp.bfloat16), "rep").astype(jnp.float32),
            lax.psum(owned_sums[8].astype(jnp.bfloat16), "rep").astype(jnp.float32),
            lax.psum(owned_sums[9].astype(jnp.bfloat16), "rep").astype(jnp.float32),
        )
        shards[layer_index] = owned_sums
    stacked_grads = tuple((jnp.stack([shards[j][i] for j in range(LAYERS)]) for i in range(10)))
    return (stream, grad_stream, grad_cond) + stacked_grads


def solution(mesh):
    in_specs = (
        P(("fsdp", "rep"), None, None),
        P(("fsdp", "rep"), None),
        P(("fsdp", "rep"), None, None),
        P(None, "fsdp", None),
        P(None, "fsdp"),
        P(None, "fsdp", None),
        P(None, "fsdp"),
        P(None, "fsdp", None),
        P(None, "fsdp"),
        P(None, "fsdp", None),
        P(None, "fsdp"),
        P(None, "fsdp", None),
        P(None, "fsdp"),
    )
    out_specs = (
        P(("fsdp", "rep"), None, None),
        P(("fsdp", "rep"), None, None),
        P(("fsdp", "rep"), None),
        P(None, "fsdp", None),
        P(None, "fsdp"),
        P(None, "fsdp", None),
        P(None, "fsdp"),
        P(None, "fsdp", None),
        P(None, "fsdp"),
        P(None, "fsdp", None),
        P(None, "fsdp"),
        P(None, "fsdp", None),
        P(None, "fsdp"),
    )
    return jax.shard_map(body, mesh=mesh, in_specs=in_specs, out_specs=out_specs, check_vma=False)
```

profile of v0, /device:TPU:0, one launch (start us, length us, event | category | flops | bytes accessed | tf_op | source)
XLA Modules:
  0.0 1179.6 jit_solution(6326753263943865538)
XLA Ops:
  20.5 39.6 %all-reduce.21 = (bf16[768]{0:T(1024)(128)(2,1)S(1)}, bf16[2304]{0:T(1024)(128)(2,1)S(1)}, bf16[384]{0:T(512)(128)(2,1)S(1)}, bf16[1536]{0:T(1024)(128)(2,1)S(1)...) all-reduce(bf16[768]{0:T(1024)(128)(2,1)S(1)} %dynamic-update-slice, ...), channel_id=5, replica_groups=mesh['fsdp'=8,'rep'=4] {'fsdp'}, use_global_device_ids=true, to_apply=%add.1 | all-reduce | flops 10752 | bytes 43008
  66.5 33.9 %all-gather.14 = bf16[1,384,384]{2,1,0:T(8,128)(2,1)} all-gather(bf16[1,48,384]{2,1,0:T(8,128)(2,1)S(1)} %get-tuple-element.118), channel_id=16, replica_groups=mesh['fsdp'=8,'rep'=4] {'fsdp'}, dimensions={1}, use_global_device_ids=true | all-gather | bytes 331776 | tf_op jit(solution)/shard_map/all_gather | solution.py:251
  100.4 31.4 %all-gather.4 = bf16[1,384,384]{2,1,0:T(8,128)(2,1)S(1)} all-gather(bf16[1,48,384]{2,1,0:T(8,128)(2,1)S(1)} %get-tuple-element.119), channel_id=6, replica_groups=mesh['fsdp'=8,'rep'=4] {'fsdp'}, dimensions={1}, use_global_device_ids=true | all-gather | bytes 331776 | tf_op jit(solution)/shard_map/all_gather | solution.py:251
  131.8 35.8 %all-gather.12 = bf16[1,384,1152]{2,1,0:T(8,128)(2,1)} all-gather(bf16[1,48,1152]{2,1,0:T(8,128)(2,1)S(1)} %get-tuple-element.110), channel_id=14, replica_groups=mesh['fsdp'=8,'rep'=4] {'fsdp'}, dimensions={1}, use_global_device_ids=true | all-gather | bytes 995328 | tf_op jit(solution)/shard_map/all_gather | solution.py:251
  167.6 35.7 %all-gather.2 = bf16[1,384,1152]{2,1,0:T(8,128)(2,1)} all-gather(bf16[1,48,1152]{2,1,0:T(8,128)(2,1)S(1)} %get-tuple-element.111), channel_id=4, replica_groups=mesh['fsdp'=8,'rep'=4] {'fsdp'}, dimensions={1}, use_global_device_ids=true | all-gather | bytes 995328 | tf_op jit(solution)/shard_map/all_gather | solution.py:251
  208.9 4.5 add_convert_fusion.1
  215.8 2.7 copy.130
  218.5 2.6 copy.129
  221.1 2.6 copy.128
  223.7 3.7 multiply_reduce_fusion.3
  232.0 3.7 convolution_convert_fusion.5
  235.8 3.1 fusion.153
  241.4 11.6 multiply_convert_fusion.3
  253.0 8.4 fusion.152
  263.2 3.2 add_convert_fusion
  271.3 2.6 copy.134
  273.9 3.0 copy.133
  276.9 3.7 multiply_reduce_fusion.2
  285.3 3.9 convolution_convert_fusion.4
  289.2 3.1 fusion.151
  295.2 11.1 multiply_convert_fusion.2
  306.4 14.5 %fusion.168 = (bf16[1536]{0:T(1024)(128)(2,1)}, bf16[8,256,1536]{2,1,0:T(8,128)(2,1)S(1)}) fusion(f32[8,256,1536]{2,1,0:T(8,128)} %get-tuple-element.146, f32[1536]{0:T(1024)} %convert_element_type.337, bf16[1,1536,384]{2,1,0:T(8,128)(2,1)} %all-gather.37.cloned.1.call-done, f32[8,256,384]{2,1,0:T(8,128)} %param.15, f32[8,384]{1,0:T(8,128)} %get-tuple-element.112), kind=kOutput, calls=%fused_computation.276 | convolution fusion | flops 2483550720 | bytes 23221248 | tf_op jit(solution)/shard_map/dot_general | solution.py:32
  320.9 5.9 multiply_reduce_fusion.9
  327.4 9.0 multiply_reduce_fusion.23
  341.8 2.8 copy.138
  344.6 9.6 bitcast_convert_fusion.2
  354.2 6.3 fusion.170
  360.5 22.9 %fusion.85 = bf16[8,6,64,256]{3,2,1,0:T(8,128)(2,1)} fusion(bf16[8,256,6,64]{1,3,2,0:T(8,128)(2,1)} %bitcast.264, f32[8,6,256,256]{2,3,1,0:T(8,128)} %fusion.170, f32[8,6,256,256]{2,3,1,0:T(8,128)} %copy-done.1, f32[8,6,256]{2,1,0:T(8,128)S(1)} %log_add_fusion), kind=kOutput, calls=%fused_computation.139 | convolution fusion | flops 431763712 | bytes 28360704 | tf_op jit(solution)/shard_map/bhqk,bqhe->bkhe/dot_general | solution.py:21
  383.4 21.4 %bitcast_convert_fusion.3 = (bf16[8,256,6,64]{1,3,2,0:T(8,128)(2,1)}, f32[8,6,64,256]{3,2,1,0:T(8,128)}) fusion(bf16[8,256,6,64]{1,3,2,0:T(8,128)(2,1)} %bitcast.262, f32[8,6,256,256]{2,3,1,0:T(8,128)} %fusion.170, f32[8,6,256,256]{2,3,1,0:T(8,128)} %copy-done.1, f32[8,6,256]{2,1,0:T(8,128)S(1)} %log_add_fusion), kind=kOutput, calls=%fused_computation.61 | convolution fusion | flops 431763712 | bytes 31506432 | tf_op jit(solution)/shard_map/bhqk,bkhe->bqhe/dot_general | solution.py:21
  407.4 2.6 copy.142
  410.0 3.0 copy.143
  413.1 6.7 fusion.65
  419.7 7.3 multiply_reduce_fusion.11
  432.9 5.9 multiply_reduce_fusion.21
  438.9 13.3 %fusion.169 = (bf16[1536]{0:T(1024)(128)(2,1)S(1)}, bf16[8,256,1536]{2,1,0:T(8,128)(2,1)S(1)}) fusion(f32[8,256,1536]{2,1,0:T(8,128)} %get-tuple-element.140, f32[1536]{0:T(1024)S(1)} %copy-done.79, bf16[1,1536,384]{2,1,0:T(8,128)(2,1)S(1)} %copy-done.97, f32[8,256,384]{2,1,0:T(8,128)S(1)} %get-tuple-element.85, f32[8,384]{1,0:T(8,128)S(1)} %get-tuple-element.120), kind=kOutput, calls=%fused_computation.277 | convolution fusion | flops 2483550720 | bytes 23221248 | tf_op jit(solution)/shard_map/dot_general | solution.py:32
  452.2 4.5 multiply_reduce_fusion.5
  463.9 3.6 convolution_convert_fusion.7
  467.9 9.1 bitcast_convert_fusion
  477.1 6.3 fusion.171
  483.4 2.7 copy.151
  486.1 22.5 %bitcast_convert_fusion.1 = (bf16[8,256,6,64]{1,3,2,0:T(8,128)(2,1)S(1)}, f32[8,6,64,256]{3,2,1,0:T(8,128)}) fusion(bf16[8,256,6,64]{1,3,2,0:T(8,128)(2,1)S(1)} %bitcast.260, f32[8,6,256,256]{2,3,1,0:T(8,128)} %fusion.171, f32[8,6,256,256]{2,3,1,0:T(8,128)} %copy-done, f32[8,6,256]{2,1,0:T(8,128)S(1)} %copy-done.32), kind=kOutput, calls=%fused_computation.57 | convolution fusion | flops 431763712 | bytes 31506432 | tf_op jit(solution)/shard_map/bhqk,bkhe->bqhe/dot_general | solution.py:21
  510.2 22.3 %fusion.82 = bf16[8,6,64,256]{3,2,1,0:T(8,128)(2,1)} fusion(bf16[8,256,6,64]{1,3,2,0:T(8,128)(2,1)S(1)} %bitcast.258, f32[8,6,256,256]{2,3,1,0:T(8,128)} %fusion.171, f32[8,6,256,256]{2,3,1,0:T(8,128)} %copy-done, f32[8,6,256]{2,1,0:T(8,128)S(1)} %copy-done.32), kind=kOutput, calls=%fused_computation.138 | convolution fusion | flops 431763712 | bytes 28360704 | tf_op jit(solution)/shard_map/bhqk,bqhe->bkhe/dot_general | solution.py:21
  532.5 2.8 copy.150
  535.3 6.1 fusion.64
  542.0 7.5 fusion.69
  549.6 8.2 fusion.73
  558.0 8.2 fusion.72
  566.3 7.6 fusion.66
  574.2 2.8 convolution_convert_fusion
  577.1 6.7 multiply_reduce_fusion.7
  583.9 2.8 convolution_convert_fusion.1
  598.4 33.9 %all-reduce.20 = (bf16[2304]{0:T(1024)(128)(2,1)S(1)}, bf16[2304]{0:T(1024)(128)(2,1)S(1)}, bf16[768]{0:T(1024)(128)(2,1)S(1)}, bf16[768]{0:T(1024)(128)(2,1)S(1...) all-reduce(bf16[2304]{0:T(1024)(128)(2,1)S(1)} %reduce_sum.477, ...), channel_id=25, replica_groups=mesh['fsdp'=8,'rep'=4] {'fsdp'}, use_global_device_ids=true, to_apply=%region_42.43.clone | all-reduce | flops 10752 | bytes 43008
  638.5 3.0 fusion.76
  641.5 4.7 multiply_add_fusion.2
  646.3 3.6 fusion.106
  649.9 31.7 %reduce-scatter.15.cloned.1.call-done = bf16[48,1152]{1,0:T(8,128)(2,1)} async-done(((bf16[384,1152]{1,0:T(8,128)(2,1)}), bf16[48,1152]{1,0:T(8,128)(2,1)}) %reduce-scatter.15.cloned.1.call-update) | async-done | bytes 110608 | tf_op jit(solution)/shard_map/reduce_scatter | solution.py:278
  681.6 66.9 %reduce-scatter.25.cloned.1.call-done = bf16[48,1536]{1,0:T(8,128)(2,1)} async-done(((bf16[384,1536]{1,0:T(8,128)(2,1)}), bf16[48,1536]{1,0:T(8,128)(2,1)}) %reduce-scatter.25.cloned.1.call-update) | async-done | bytes 147472 | tf_op jit(solution)/shard_map/reduce_scatter | solution.py:290
  748.5 67.0 %reduce-scatter.29.cloned.1.call-done = bf16[192,384]{1,0:T(8,128)(2,1)} async-done(((bf16[1536,384]{1,0:T(8,128)(2,1)}), bf16[192,384]{1,0:T(8,128)(2,1)}) %reduce-scatter.29.cloned.1.call-update) | async-done | bytes 147472 | tf_op jit(solution)/shard_map/reduce_scatter | solution.py:296
  815.6 67.1 %reduce-scatter.27.cloned.1.call-done = bf16[192,384]{1,0:T(8,128)(2,1)} async-done(((bf16[1536,384]{1,0:T(8,128)(2,1)}), bf16[192,384]{1,0:T(8,128)(2,1)}) %reduce-scatter.27.cloned.1.call-update) | async-done | bytes 147472 | tf_op jit(solution)/shard_map/reduce_scatter | solution.py:296
  882.7 67.0 %reduce-scatter.23.cloned.1.call-done = bf16[48,1536]{1,0:T(8,128)(2,1)} async-done(((bf16[384,1536]{1,0:T(8,128)(2,1)}), bf16[48,1536]{1,0:T(8,128)(2,1)}) %reduce-scatter.23.cloned.1.call-update) | async-done | bytes 147472 | tf_op jit(solution)/shard_map/reduce_scatter | solution.py:290
  949.6 69.0 %reduce-scatter.13.cloned.1.call-done = bf16[48,2304]{1,0:T(8,128)(2,1)} async-done(((bf16[384,2304]{1,0:T(8,128)(2,1)}), bf16[48,2304]{1,0:T(8,128)(2,1)}) %reduce-scatter.13.cloned.1.call-update) | async-done | bytes 221200 | tf_op jit(solution)/shard_map/reduce_scatter | solution.py:272
  1018.6 68.8 %reduce-scatter.11.cloned.1.call-done = bf16[48,2304]{1,0:T(8,128)(2,1)} async-done(((bf16[384,2304]{1,0:T(8,128)(2,1)}), bf16[48,2304]{1,0:T(8,128)(2,1)}) %reduce-scatter.11.cloned.1.call-update) | async-done | bytes 221200 | tf_op jit(solution)/shard_map/reduce_scatter | solution.py:272
  1087.4 34.4 %all-reduce.27.cloned.1.call-done = (bf16[1,288]{1,0:T(2,128)(2,1)}, bf16[1,288]{1,0:T(2,128)(2,1)}, bf16[1,96]{1,0:T(2,128)(2,1)}, bf16[1,96]{1,0:T(2,128)(2,1)...) async-done(((bf16[1,288]{1,0:T(2,128)(2,1)}, ...) | async-done | bytes 76432 | tf_op jit(solution)/shard_map/psum | solution.py:305
  1129.4 35.8 %all-reduce.29.cloned.1.call-done = (bf16[1,48,2304]{2,1,0:T(8,128)(2,1)}, bf16[1,48,2304]{2,1,0:T(8,128)(2,1)}, bf16[1,48,1152]{2,1,0:T(8,128)(2,1)}, bf16[1,48...) async-done(((bf16[1,48,2304]{2,1,0:T(8,128)(2,1)}, ...) | async-done | bytes 1253392 | tf_op jit(solution)/shard_map/psum | solution.py:304
  (389 shorter events, 100.7 us)
Async XLA Ops:
  7.2 7.7 copy-start.88
  7.2 10.9 copy-start.90
  7.2 10.9 copy-start.91
  7.2 10.9 copy-start.87
  7.2 10.9 copy-start.92
  7.2 10.9 copy-start.85
  7.2 11.0 copy-start.47
  7.3 57.5 %copy-start.2 = (f32[8,256,384]{2,1,0:T(8,128)S(1)}, f32[8,256,384]{2,1,0:T(8,128)}, u32[]{:S(2)}) copy-start(f32[8,256,384]{2,1,0:T(8,128)} %param.13) | copy-start | bytes 9437188
  7.3 196.7 %all-gather.27.cloned.1.call-start = ((), (), s32[]{:S(2)}) async-start(), calls=%async_computation.20 | async-start | bytes 1990656 | tf_op jit(solution)/shard_map/all_gather | solution.py:251
  9.3 197.1 %all-gather.33.cloned.1.call-start = ((), (), s32[]{:S(2)}) async-start(), calls=%async_computation.23 | async-start | bytes 1990656 | tf_op jit(solution)/shard_map/all_gather | solution.py:251
  10.1 231.2 %all-gather.29.cloned.1.call-start = ((), (), s32[]{:S(2)}) async-start(), calls=%async_computation.21 | async-start | bytes 1327104 | tf_op jit(solution)/shard_map/all_gather | solution.py:251
  11.9 241.1 %all-gather.31.cloned.1.call-start = ((), (), s32[]{:S(2)}) async-start(), calls=%async_computation.22 | async-start | bytes 1327104 | tf_op jit(solution)/shard_map/all_gather | solution.py:251
  13.7 281.6 %all-gather.35.cloned.1.call-start = ((), (), s32[]{:S(2)}) async-start(), calls=%async_computation.24 | async-start | bytes 1327104 | tf_op jit(solution)/shard_map/all_gather | solution.py:251
  14.3 292.1 %all-gather.37.cloned.1.call-start = ((), (), s32[]{:S(2)}) async-start(), calls=%async_computation.25 | async-start | bytes 1327104 | tf_op jit(solution)/shard_map/all_gather | solution.py:251
  14.8 631.4 %reduce-scatter.21.cloned.1.call-start = ((), (), s32[]{:S(2)}) async-start(), calls=%async_computation.15 | async-start | bytes 331776 | tf_op jit(solution)/shard_map/reduce_scatter | solution.py:284
  18.2 188.2 %copy-start.36 = (bf16[8,384]{1,0:T(8,128)(2,1)}, bf16[8,384]{1,0:T(8,128)(2,1)S(1)}, u32[]{:S(2)}) copy-start(bf16[8,384]{1,0:T(8,128)(2,1)S(1)} %multiply_convert_fusion.12) | copy-start | bytes 18436
  65.2 143.7 %copy-start.40 = (f32[8,256]{1,0:T(8,128)}, f32[8,256]{1,0:T(8,128)S(1)}, u32[]{:S(2)}) copy-start(f32[8,256]{1,0:T(8,128)S(1)} %broadcast_multiply_fusion.11) | copy-start | bytes 24580
  65.2 138.1 %copy-start.71 = (bf16[1,768]{1,0:T(2,128)(2,1)S(1)}, bf16[1,768]{1,0:T(2,128)(2,1)}, u32[]{:S(2)}) copy-start(bf16[1,768]{1,0:T(2,128)(2,1)} %reshape.387) | copy-start | bytes 4612
  65.2 138.1 %copy-start.72 = (bf16[1,768]{1,0:T(2,128)(2,1)S(1)}, bf16[1,768]{1,0:T(2,128)(2,1)}, u32[]{:S(2)}) copy-start(bf16[1,768]{1,0:T(2,128)(2,1)} %reshape.402) | copy-start | bytes 4612
  100.4 108.5 %copy-start.53 = (f32[8,256]{1,0:T(8,128)S(1)}, f32[8,256]{1,0:T(8,128)}, u32[]{:S(2)}) copy-start(f32[8,256]{1,0:T(8,128)} %add_rsqrt_fusion.3) | copy-start | bytes 24580
  131.8 103.9 %copy-start.27 = (bf16[1,384,384]{2,1,0:T(8,128)(2,1)}, bf16[1,384,384]{2,1,0:T(8,128)(2,1)S(1)}, u32[]{:S(2)}) copy-start(bf16[1,384,384]{2,1,0:T(8,128)(2,1)S(1)} %all-gather.4) | copy-start | bytes 884740
  206.4 7.1 copy-start.64
  206.4 29.3 %copy-start.34 = (f32[8,384]{1,0:T(8,128)}, f32[8,384]{1,0:T(8,128)S(1)}, u32[]{:S(2)}) copy-start(f32[8,384]{1,0:T(8,128)S(1)} %get-tuple-element.125) | copy-start | bytes 36868
  206.4 34.9 %copy-start.45 = (f32[8,384]{1,0:T(8,128)}, f32[8,384]{1,0:T(8,128)S(1)}, u32[]{:S(2)}) copy-start(f32[8,384]{1,0:T(8,128)S(1)} %get-tuple-element.122) | copy-start | bytes 36868
  238.9 14.0 %copy-start.38 = (f32[8,256]{1,0:T(8,128)}, f32[8,256]{1,0:T(8,128)S(1)}, u32[]{:S(2)}) copy-start(f32[8,256]{1,0:T(8,128)S(1)} %broadcast_multiply_fusion.10) | copy-start | bytes 24580
  241.3 11.7 copy-start.49
  241.4 11.6 copy-start.5
  241.4 11.6 copy-start.77
  306.3 14.5 %copy-start.17 = (f32[8,256,384]{2,1,0:T(8,128)S(1)}, f32[8,256,384]{2,1,0:T(8,128)}, u32[]{:S(2)}) copy-start(f32[8,256,384]{2,1,0:T(8,128)} %copy-done.16) | copy-start | bytes 9437188
  306.3 14.5 %copy-start.56 = (f32[8,256]{1,0:T(8,128)S(1)}, f32[8,256]{1,0:T(8,128)}, u32[]{:S(2)}) copy-start(f32[8,256]{1,0:T(8,128)} %copy-done.55) | copy-start | bytes 24580
  306.3 14.5 %copy-start.67 = (f32[8,384]{1,0:T(8,128)S(1)}, f32[8,384]{1,0:T(8,128)}, u32[]{:S(2)}) copy-start(f32[8,384]{1,0:T(8,128)} %get-tuple-element.114) | copy-start | bytes 36868
  306.3 14.5 %copy-start.80 = (f32[8,256]{1,0:T(8,128)S(1)}, f32[8,256]{1,0:T(8,128)}, u32[]{:S(2)}) copy-start(f32[8,256]{1,0:T(8,128)} %add_rsqrt_fusion) | copy-start | bytes 24580
  306.3 14.5 %copy-start.99 = (bf16[1,384,1536]{2,1,0:T(8,128)(2,1)S(1)}, bf16[1,384,1536]{2,1,0:T(8,128)(2,1)}, u32[]{:S(2)}) copy-start(bf16[1,384,1536]{2,1,0:T(8,128)(2,1)} %all-gather.35.cloned.1.call-done) | copy-start | bytes 3538948
  344.6 9.6 copy-start.9
  344.6 9.6 copy-start.15
  419.7 7.3 copy-start.11
  432.8 213.4 %reduce-scatter.19.cloned.1.call-start = ((), (), s32[]{:S(2)}) async-start(), calls=%async_computation.14 | async-start | bytes 331776 | tf_op jit(solution)/shard_map/reduce_scatter | solution.py:284
  438.8 18.0 %copy-start.19 = (f32[8,256,384]{2,1,0:T(8,128)}, f32[8,256,384]{2,1,0:T(8,128)S(1)}, u32[]{:S(2)}) copy-start(f32[8,256,384]{2,1,0:T(8,128)S(1)} %get-tuple-element.85) | copy-start | bytes 9437188
  438.8 13.3 %copy-start.39 = (f32[8,256]{1,0:T(8,128)S(1)}, f32[8,256]{1,0:T(8,128)}, u32[]{:S(2)}) copy-start(f32[8,256]{1,0:T(8,128)} %copy-done.38) | copy-start | bytes 24580
  438.8 13.3 %copy-start.46 = (f32[8,384]{1,0:T(8,128)S(1)}, f32[8,384]{1,0:T(8,128)}, u32[]{:S(2)}) copy-start(f32[8,384]{1,0:T(8,128)} %copy-done.45) | copy-start | bytes 36868
  438.8 13.3 %copy-start.50 = (f32[8,256]{1,0:T(8,128)S(1)}, f32[8,256]{1,0:T(8,128)}, u32[]{:S(2)}) copy-start(f32[8,256]{1,0:T(8,128)} %copy-done.49) | copy-start | bytes 24580
  438.9 13.3 %copy-start.96 = (bf16[1,384,1536]{2,1,0:T(8,128)(2,1)S(1)}, bf16[1,384,1536]{2,1,0:T(8,128)(2,1)}, u32[]{:S(2)}) copy-start(bf16[1,384,1536]{2,1,0:T(8,128)(2,1)} %all-gather.29.cloned.1.call-done) | copy-start | bytes 3538948
  467.6 182.3 %reduce-scatter.17.cloned.1.call-start = ((), (), s32[]{:S(2)}) async-start(), calls=%async_computation.13 | async-start | bytes 995328 | tf_op jit(solution)/shard_map/reduce_scatter | solution.py:278
  467.8 9.2 copy-start.14
  477.0 204.6 %reduce-scatter.15.cloned.1.call-start = ((), (), s32[]{:S(2)}) async-start(), calls=%async_computation.12 | async-start | bytes 995328 | tf_op jit(solution)/shard_map/reduce_scatter | solution.py:278
  510.2 25.1 %copy-start.41 = (f32[8,256]{1,0:T(8,128)S(1)}, f32[8,256]{1,0:T(8,128)}, u32[]{:S(2)}) copy-start(f32[8,256]{1,0:T(8,128)} %copy-done.40) | copy-start | bytes 24580
  510.2 25.1 %copy-start.44 = (f32[8,384]{1,0:T(8,128)S(1)}, f32[8,384]{1,0:T(8,128)}, u32[]{:S(2)}) copy-start(f32[8,384]{1,0:T(8,128)} %copy-done.43) | copy-start | bytes 36868
  510.2 25.1 %copy-start.54 = (f32[8,256]{1,0:T(8,128)S(1)}, f32[8,256]{1,0:T(8,128)}, u32[]{:S(2)}) copy-start(f32[8,256]{1,0:T(8,128)} %add_rsqrt_fusion.3) | copy-start | bytes 24580
  510.2 25.1 %copy-start.65 = (f32[8,384]{1,0:T(8,128)S(1)}, f32[8,384]{1,0:T(8,128)}, u32[]{:S(2)}) copy-start(f32[8,384]{1,0:T(8,128)} %copy-done.64) | copy-start | bytes 36868
  541.5 8.1 copy-start.63
  541.5 207.0 %reduce-scatter.25.cloned.1.call-start = ((), (), s32[]{:S(2)}) async-start(), calls=%async_computation.17 | async-start | bytes 1327104 | tf_op jit(solution)/shard_map/reduce_scatter | solution.py:290
  549.6 266.0 %reduce-scatter.29.cloned.1.call-start = ((), (), s32[]{:S(2)}) async-start(), calls=%async_computation.19 | async-start | bytes 1327104 | tf_op jit(solution)/shard_map/reduce_scatter | solution.py:296
  557.9 8.4 copy-start.61
  557.9 324.8 %reduce-scatter.27.cloned.1.call-start = ((), (), s32[]{:S(2)}) async-start(), calls=%async_computation.18 | async-start | bytes 1327104 | tf_op jit(solution)/shard_map/reduce_scatter | solution.py:296
  566.2 8.0 copy-start.76
  566.2 8.0 copy-start.74
  566.2 8.0 copy-start.73
  566.2 8.0 copy-start.75
  566.2 8.0 copy-start.37
  566.3 383.4 %reduce-scatter.23.cloned.1.call-start = ((), (), s32[]{:S(2)}) async-start(), calls=%async_computation.16 | async-start | bytes 1327104 | tf_op jit(solution)/shard_map/reduce_scatter | solution.py:290
  573.9 444.7 %reduce-scatter.13.cloned.1.call-start = ((), (), s32[]{:S(2)}) async-start(), calls=%async_computation.11 | async-start | bytes 1990656 | tf_op jit(solution)/shard_map/reduce_scatter | solution.py:272
  577.1 510.3 %reduce-scatter.11.cloned.1.call-start = ((), (), s32[]{:S(2)}) async-start(), calls=%async_computation.10 | async-start | bytes 1990656 | tf_op jit(solution)/shard_map/reduce_scatter | solution.py:272
  586.7 535.1 %all-reduce.27.cloned.1.call-start = ((), (), s32[]{:S(2)}) async-start(), calls=%async_computation.26 | async-start | bytes 163840 | tf_op jit(solution)/shard_map/psum | solution.py:305
  646.2 519.0 %all-reduce.29.cloned.1.call-start = ((), (), s32[]{:S(2)}) async-start(), calls=%async_computation.27 | async-start | bytes 2506752 | tf_op jit(solution)/shard_map/psum | solution.py:304
  (56 other events, 225.2 us)
Sparse Core Ops, SparseCore 0:
  10.8 49.4 all-gather.26
  63.0 47.2 all-gather.32
  113.1 45.0 all-gather.28
  160.2 43.9 all-gather.30
  206.8 39.9 all-gather.34
  248.8 39.7 all-gather.36
  432.9 56.9 reduce-scatter.20
  493.7 58.5 reduce-scatter.18
  556.3 61.1 reduce-scatter.16
  620.7 60.8 reduce-scatter.14
  685.0 63.4 reduce-scatter.24
  751.8 63.7 reduce-scatter.28
  818.9 63.6 reduce-scatter.26
  885.9 63.6 reduce-scatter.22
  952.9 65.6 reduce-scatter.12
  1021.9 65.4 reduce-scatter.10
  1091.6 30.2 all-reduce.26
  1124.6 40.5 all-reduce.28
where the time goes:
time: 1190 us; the launch traced here: 1180 us
  waiting for transfers between devices  510 us (43%)
  matrix products  311 us (26%)
  blocking collectives  210 us (18%)
  local copies, waits for them, and re-layouts  74.5 us (6%)
  other arithmetic  51.7 us (4%)
  between operations  21.2 us (2%)
    reduce_scatter x2, waiting for transfers between devices, body(): lax.psum_scatter(gradients[0].astype(jnp.bfloat16), 'fsdp', scatter_dimen...  138 us
    all_gather x4, blocking collectives, body(): lax.all_gather(as_sent(owned_rows), 'fsdp', axis=0, tiled=True)  137 us
    dot_general x12, matrix products, pair_product(): return jnp.einsum(form, left, right, preferred_element_type=jnp.float32)  136 us
    reduce_scatter x2, waiting for transfers between devices, body(): lax.psum_scatter(gradients[8].astype(jnp.bfloat16), 'fsdp', scatter_dimen...  134 us
    reduce_scatter x2, waiting for transfers between devices, body(): lax.psum_scatter(gradients[6].astype(jnp.bfloat16), 'fsdp', scatter_dimen...  134 us
    unnamed x2, blocking collectives  73.5 us
    dot_general x8, matrix products, matmul_back(): lax.dot_general(flattened, weight, (((1,), (1,)), ((), ())), preferred_el...  55.6 us
    dot_general x8, matrix products, matmul(): result = jnp.dot(flattened, weight, preferred_element_type=jnp.float32)  53.9 us
  transfers between devices with their start and end apart: 18, of which 9 were waited for; matrix products, arithmetic and copies ran while one was open for 25% of the time, Pallas kernels for 0%

commit v1 on v0

--- a/solution.py
+++ b/solution.py
@@ -300,9 +300,13 @@
                 gradients[9].astype(jnp.bfloat16), "fsdp", scatter_dimension=0, tiled=True
             ).astype(jnp.float32),
         )
+
+        def step_on_scales_on_mesh(x0):
+            return lax.all_gather(x0, axis_name="rep").sum(axis=0)
+
         owned_sums = (
             lax.psum(owned_sums[0].astype(jnp.bfloat16), "rep").astype(jnp.float32),
-            lax.psum(owned_sums[1].astype(jnp.bfloat16), "rep").astype(jnp.float32),
+            step_on_scales_on_mesh(owned_sums[1].astype(jnp.bfloat16)).astype(jnp.float32),
             lax.psum(owned_sums[2].astype(jnp.bfloat16), "rep").astype(jnp.float32),
             lax.psum(owned_sums[3].astype(jnp.bfloat16), "rep").astype(jnp.float32),
             lax.psum(owned_sums[4].astype(jnp.bfloat16), "rep").astype(jnp.float32),

time: 1190 us -> 1270 us (1.067)
  waiting for transfers between devices: 510 us -> 597 us
    reduce_scatter x2, waiting for transfers between devices: 31.7 us -> 102 us  [body(): lax.psum_scatter(gradients[2].astype(jnp.bfloat16), 'fsdp', scatter_dimen...]
    reduce_scatter x2, waiting for transfers between devices: 0.01 us -> 53.6 us  [body(): lax.psum_scatter(gradients[4].astype(jnp.bfloat16), 'fsdp', scatter_dimen...]
    psum x1 -> x0, waiting for transfers between devices: 34.4 us -> none  [body(): lax.psum(owned_sums[1].astype(jnp.bfloat16), 'rep').astype(jnp.float32)]
  transfers between devices with their start and end apart: 18 -> 18, of which waited for: 9 -> 10; matrix products, arithmetic and copies ran while one was open for 25% -> 16% of each run, Pallas kernels for 0% -> 0%
where the time goes in v1:
time: 1270 us; the launch traced here: 1260 us
  waiting for transfers between devices  597 us (47%)
  matrix products  313 us (25%)
  blocking collectives  209 us (16%)
  local copies, waits for them, and re-layouts  77.9 us (6%)
  other arithmetic  43.9 us (3%)
  between operations  22 us (2%)
    reduce_scatter x2, waiting for transfers between devices, body(): lax.psum_scatter(gradients[0].astype(jnp.bfloat16), 'fsdp', scatter_dimen...  138 us
    dot_general x12, matrix products, pair_product(): return jnp.einsum(form, left, right, preferred_element_type=jnp.float32)  137 us
    all_gather x4, blocking collectives, body(): lax.all_gather(as_sent(owned_rows), 'fsdp', axis=0, tiled=True)  136 us
    reduce_scatter x2, waiting for transfers between devices, body(): lax.psum_scatter(gradients[8].astype(jnp.bfloat16), 'fsdp', scatter_dimen...  134 us
    reduce_scatter x2, waiting for transfers between devices, body(): lax.psum_scatter(gradients[6].astype(jnp.bfloat16), 'fsdp', scatter_dimen...  134 us
    reduce_scatter x2, waiting for transfers between devices, body(): lax.psum_scatter(gradients[2].astype(jnp.bfloat16), 'fsdp', scatter_dimen...  102 us
    unnamed x2, blocking collectives  73.5 us
    dot_general x8, matrix products, matmul_back(): lax.dot_general(flattened, weight, (((1,), (1,)), ((), ())), preferred_el...  56.2 us
  transfers between devices with their start and end apart: 18, of which 10 were waited for; matrix products, arithmetic and copies ran while one was open for 16% of the time, Pallas kernels for 0%

profile of v1, /device:TPU:0, one launch (start us, length us, event | category | flops | bytes accessed | tf_op | source)
XLA Modules:
  0.0 1263.8 jit_solution(17372484262797782632)
XLA Ops:
  24.4 39.7 %all-reduce.23 = (bf16[768]{0:T(1024)(128)(2,1)S(1)}, bf16[2304]{0:T(1024)(128)(2,1)S(1)}, bf16[384]{0:T(512)(128)(2,1)S(1)}, bf16[1536]{0:T(1024)(128)(2,1)S(1)...) all-reduce(bf16[768]{0:T(1024)(128)(2,1)S(1)} %dynamic-update-slice, ...), channel_id=5, replica_groups=mesh['fsdp'=8,'rep'=4] {'fsdp'}, use_global_device_ids=true, to_apply=%add.1 | all-reduce | flops 10752 | bytes 43008
  69.9 33.5 %all-gather.14 = bf16[1,384,384]{2,1,0:T(8,128)(2,1)} all-gather(bf16[1,48,384]{2,1,0:T(8,128)(2,1)S(1)} %get-tuple-element.118), channel_id=16, replica_groups=mesh['fsdp'=8,'rep'=4] {'fsdp'}, dimensions={1}, use_global_device_ids=true | all-gather | bytes 331776 | tf_op jit(solution)/shard_map/all_gather | solution.py:251
  103.4 31.3 %all-gather.4 = bf16[1,384,384]{2,1,0:T(8,128)(2,1)S(1)} all-gather(bf16[1,48,384]{2,1,0:T(8,128)(2,1)S(1)} %get-tuple-element.119), channel_id=6, replica_groups=mesh['fsdp'=8,'rep'=4] {'fsdp'}, dimensions={1}, use_global_device_ids=true | all-gather | bytes 331776 | tf_op jit(solution)/shard_map/all_gather | solution.py:251
  134.7 35.5 %all-gather.12 = bf16[1,384,1152]{2,1,0:T(8,128)(2,1)} all-gather(bf16[1,48,1152]{2,1,0:T(8,128)(2,1)S(1)} %get-tuple-element.110), channel_id=14, replica_groups=mesh['fsdp'=8,'rep'=4] {'fsdp'}, dimensions={1}, use_global_device_ids=true | all-gather | bytes 995328 | tf_op jit(solution)/shard_map/all_gather | solution.py:251
  170.2 35.3 %all-gather.2 = bf16[1,384,1152]{2,1,0:T(8,128)(2,1)} all-gather(bf16[1,48,1152]{2,1,0:T(8,128)(2,1)S(1)} %get-tuple-element.111), channel_id=4, replica_groups=mesh['fsdp'=8,'rep'=4] {'fsdp'}, dimensions={1}, use_global_device_ids=true | all-gather | bytes 995328 | tf_op jit(solution)/shard_map/all_gather | solution.py:251
  211.0 4.9 add_convert_fusion.1
  218.3 2.7 copy.130
  226.2 3.7 multiply_reduce_fusion.3
  234.5 3.7 convolution_convert_fusion.5
  238.3 3.1 fusion.153
  243.8 11.5 multiply_convert_fusion.3
  255.4 8.5 fusion.152
  265.7 3.2 add_convert_fusion
  276.5 2.8 copy.133
  279.3 3.7 multiply_reduce_fusion.2
  287.6 3.9 convolution_convert_fusion.4
  291.6 3.1 fusion.151
  297.5 11.1 multiply_convert_fusion.2
  308.6 14.8 %fusion.168 = (bf16[1536]{0:T(1024)(128)(2,1)}, bf16[8,256,1536]{2,1,0:T(8,128)(2,1)S(1)}) fusion(f32[8,256,1536]{2,1,0:T(8,128)} %get-tuple-element.146, f32[1536]{0:T(1024)} %convert_element_type.363, bf16[1,1536,384]{2,1,0:T(8,128)(2,1)} %all-gather.39.cloned.1.call-done, f32[8,256,384]{2,1,0:T(8,128)} %param.15, f32[8,384]{1,0:T(8,128)} %get-tuple-element.112), kind=kOutput, calls=%fused_computation.276 | convolution fusion | flops 2483550720 | bytes 23221248 | tf_op jit(solution)/shard_map/dot_general | solution.py:32
  323.5 5.9 multiply_reduce_fusion.9
  330.0 9.0 multiply_reduce_fusion.23
  344.3 2.7 copy.138
  347.1 9.6 bitcast_convert_fusion.2
  356.7 6.3 fusion.170
  363.0 22.9 %fusion.85 = bf16[8,6,64,256]{3,2,1,0:T(8,128)(2,1)} fusion(bf16[8,256,6,64]{1,3,2,0:T(8,128)(2,1)} %bitcast.265, f32[8,6,256,256]{2,3,1,0:T(8,128)} %fusion.170, f32[8,6,256,256]{2,3,1,0:T(8,128)} %copy-done.1, f32[8,6,256]{2,1,0:T(8,128)S(1)} %log_add_fusion), kind=kOutput, calls=%fused_computation.139 | convolution fusion | flops 431763712 | bytes 28360704 | tf_op jit(solution)/shard_map/bhqk,bqhe->bkhe/dot_general | solution.py:21
  385.9 21.4 %bitcast_convert_fusion.3 = (bf16[8,256,6,64]{1,3,2,0:T(8,128)(2,1)}, f32[8,6,64,256]{3,2,1,0:T(8,128)}) fusion(bf16[8,256,6,64]{1,3,2,0:T(8,128)(2,1)} %bitcast.263, f32[8,6,256,256]{2,3,1,0:T(8,128)} %fusion.170, f32[8,6,256,256]{2,3,1,0:T(8,128)} %copy-done.1, f32[8,6,256]{2,1,0:T(8,128)S(1)} %log_add_fusion), kind=kOutput, calls=%fused_computation.61 | convolution fusion | flops 431763712 | bytes 31506432 | tf_op jit(solution)/shard_map/bhqk,bkhe->bqhe/dot_general | solution.py:21
  410.0 2.6 copy.142
  412.6 2.6 copy.143
  415.3 7.2 multiply_reduce_fusion.11
  422.6 2.6 multiply_reduce_fusion.21
  425.3 13.9 %fusion.169 = (bf16[1536]{0:T(1024)(128)(2,1)}, bf16[8,256,1536]{2,1,0:T(8,128)(2,1)S(1)}) fusion(f32[8,256,1536]{2,1,0:T(8,128)} %get-tuple-element.140, f32[1536]{0:T(1024)S(1)} %copy-done.88, bf16[1,1536,384]{2,1,0:T(8,128)(2,1)S(1)} %copy-done.110, f32[8,256,384]{2,1,0:T(8,128)S(1)} %get-tuple-element.85, f32[8,384]{1,0:T(8,128)S(1)} %copy-done.52), kind=kOutput, calls=%fused_computation.277 | convolution fusion | flops 2483550720 | bytes 23221248 | tf_op jit(solution)/shard_map/dot_general | solution.py:32
  439.2 4.5 multiply_reduce_fusion.5
  443.7 2.7 multiply_reduce_fusion.20
  451.8 9.3 bitcast_convert_fusion
  461.1 6.3 fusion.171
  467.4 22.8 %fusion.82 = bf16[8,6,64,256]{3,2,1,0:T(8,128)(2,1)} fusion(bf16[8,256,6,64]{1,3,2,0:T(8,128)(2,1)} %bitcast.261, f32[8,6,256,256]{2,3,1,0:T(8,128)} %fusion.171, f32[8,6,256,256]{2,3,1,0:T(8,128)} %copy-done, f32[8,6,256]{2,1,0:T(8,128)S(1)} %copy-done.40), kind=kOutput, calls=%fused_computation.138 | convolution fusion | flops 431763712 | bytes 28360704 | tf_op jit(solution)/shard_map/bhqk,bqhe->bkhe/dot_general | solution.py:21
  490.2 22.8 %bitcast_convert_fusion.1 = (bf16[8,256,6,64]{1,3,2,0:T(8,128)(2,1)}, f32[8,6,64,256]{3,2,1,0:T(8,128)}) fusion(bf16[8,256,6,64]{1,3,2,0:T(8,128)(2,1)S(1)} %bitcast.259, f32[8,6,256,256]{2,3,1,0:T(8,128)} %fusion.171, f32[8,6,256,256]{2,3,1,0:T(8,128)} %copy-done, f32[8,6,256]{2,1,0:T(8,128)S(1)} %copy-done.40), kind=kOutput, calls=%fused_computation.57 | convolution fusion | flops 431763712 | bytes 31506432 | tf_op jit(solution)/shard_map/bhqk,bkhe->bqhe/dot_general | solution.py:21
  518.4 2.8 copy.151
  524.1 2.7 copy.150
  526.8 2.9 bitcast_reduce_fusion.1
  529.8 6.4 multiply_reduce_fusion.7
  539.4 3.6 convolution_convert_fusion.7
  543.1 33.9 %all-reduce.22 = (bf16[2304]{0:T(1024)(128)(2,1)S(1)}, bf16[2304]{0:T(1024)(128)(2,1)S(1)}, bf16[768]{0:T(1024)(128)(2,1)S(1)}, bf16[768]{0:T(1024)(128)(2,1)S(1...) all-reduce(bf16[2304]{0:T(1024)(128)(2,1)S(1)} %reduce_sum.502, ...), channel_id=27, replica_groups=mesh['fsdp'=8,'rep'=4] {'fsdp'}, use_global_device_ids=true, to_apply=%region_42.43.clone | all-reduce | flops 10752 | bytes 43008
  582.5 53.6 %reduce-scatter.19.cloned.1.call-done = bf16[48,384]{1,0:T(8,128)(2,1)} async-done(((bf16[384,384]{1,0:T(8,128)(2,1)}), bf16[48,384]{1,0:T(8,128)(2,1)}) %reduce-scatter.19.cloned.1.call-update) | async-done | bytes 36880 | tf_op jit(solution)/shard_map/reduce_scatter | solution.py:284
  636.2 6.7 fusion.65
  643.0 6.4 fusion.64
  649.5 7.6 fusion.69
  657.1 8.2 fusion.73
  665.4 8.3 fusion.72
  673.8 7.6 fusion.66
  681.7 2.8 convolution_convert_fusion
  684.6 2.8 convolution_convert_fusion.1
  687.5 3.1 fusion.76
  690.6 3.6 fusion.106
  694.2 5.1 multiply_add_fusion.2
  700.9 37.4 %reduce-scatter.17.cloned.1.call-done = bf16[48,1152]{1,0:T(8,128)(2,1)} async-done(((bf16[384,1152]{1,0:T(8,128)(2,1)}), bf16[48,1152]{1,0:T(8,128)(2,1)}) %reduce-scatter.17.cloned.1.call-update) | async-done | bytes 110608 | tf_op jit(solution)/shard_map/reduce_scatter | solution.py:278
  738.3 64.4 %reduce-scatter.15.cloned.1.call-done = bf16[48,1152]{1,0:T(8,128)(2,1)} async-done(((bf16[384,1152]{1,0:T(8,128)(2,1)}), bf16[48,1152]{1,0:T(8,128)(2,1)}) %reduce-scatter.15.cloned.1.call-update) | async-done | bytes 110608 | tf_op jit(solution)/shard_map/reduce_scatter | solution.py:278
  802.7 66.7 %reduce-scatter.25.cloned.1.call-done = bf16[48,1536]{1,0:T(8,128)(2,1)} async-done(((bf16[384,1536]{1,0:T(8,128)(2,1)}), bf16[48,1536]{1,0:T(8,128)(2,1)}) %reduce-scatter.25.cloned.1.call-update) | async-done | bytes 147472 | tf_op jit(solution)/shard_map/reduce_scatter | solution.py:290
  869.5 67.1 %reduce-scatter.29.cloned.1.call-done = bf16[192,384]{1,0:T(8,128)(2,1)} async-done(((bf16[1536,384]{1,0:T(8,128)(2,1)}), bf16[192,384]{1,0:T(8,128)(2,1)}) %reduce-scatter.29.cloned.1.call-update) | async-done | bytes 147472 | tf_op jit(solution)/shard_map/reduce_scatter | solution.py:296
  936.6 67.0 %reduce-scatter.27.cloned.1.call-done = bf16[192,384]{1,0:T(8,128)(2,1)} async-done(((bf16[1536,384]{1,0:T(8,128)(2,1)}), bf16[192,384]{1,0:T(8,128)(2,1)}) %reduce-scatter.27.cloned.1.call-update) | async-done | bytes 147472 | tf_op jit(solution)/shard_map/reduce_scatter | solution.py:296
  1003.5 67.0 %reduce-scatter.23.cloned.1.call-done = bf16[48,1536]{1,0:T(8,128)(2,1)} async-done(((bf16[384,1536]{1,0:T(8,128)(2,1)}), bf16[48,1536]{1,0:T(8,128)(2,1)}) %reduce-scatter.23.cloned.1.call-update) | async-done | bytes 147472 | tf_op jit(solution)/shard_map/reduce_scatter | solution.py:290
  1070.5 69.3 %reduce-scatter.13.cloned.1.call-done = bf16[48,2304]{1,0:T(8,128)(2,1)} async-done(((bf16[384,2304]{1,0:T(8,128)(2,1)}), bf16[48,2304]{1,0:T(8,128)(2,1)}) %reduce-scatter.13.cloned.1.call-update) | async-done | bytes 221200 | tf_op jit(solution)/shard_map/reduce_scatter | solution.py:272
  1139.8 68.8 %reduce-scatter.11.cloned.1.call-done = bf16[48,2304]{1,0:T(8,128)(2,1)} async-done(((bf16[384,2304]{1,0:T(8,128)(2,1)}), bf16[48,2304]{1,0:T(8,128)(2,1)}) %reduce-scatter.11.cloned.1.call-update) | async-done | bytes 221200 | tf_op jit(solution)/shard_map/reduce_scatter | solution.py:272
  1215.6 33.7 %all-reduce.31.cloned.1.call-done = (bf16[1,48,2304]{2,1,0:T(8,128)(2,1)}, bf16[1,48,2304]{2,1,0:T(8,128)(2,1)}, bf16[1,48,1152]{2,1,0:T(8,128)(2,1)}, bf16[1,48...) async-done(((bf16[1,48,2304]{2,1,0:T(8,128)(2,1)}, ...) | async-done | bytes 1253392 | tf_op jit(solution)/shard_map/psum | solution.py:308
  (426 shorter events, 101.3 us)
Async XLA Ops:
  7.2 7.7 copy-start.113
  7.2 9.0 copy-start.101
  7.2 14.7 %copy-start.103 = (bf16[2,96]{1,0:T(2,128)(2,1)S(1)}, bf16[2,96]{1,0:T(2,128)(2,1)}, u32[]{:S(2)}) copy-start(bf16[2,96]{1,0:T(2,128)(2,1)} %param.19) | copy-start | bytes 1156
  7.2 14.7 %copy-start.104 = (bf16[2,48]{1,0:T(2,128)(2,1)S(1)}, bf16[2,48]{1,0:T(2,128)(2,1)}, u32[]{:S(2)}) copy-start(bf16[2,48]{1,0:T(2,128)(2,1)} %param.21) | copy-start | bytes 580
  7.2 14.8 %copy-start.100 = (bf16[2,192]{1,0:T(2,128)(2,1)S(1)}, bf16[2,192]{1,0:T(2,128)(2,1)}, u32[]{:S(2)}) copy-start(bf16[2,192]{1,0:T(2,128)(2,1)} %param.23) | copy-start | bytes 2308
  7.2 14.8 %copy-start.105 = (bf16[2,48]{1,0:T(2,128)(2,1)S(1)}, bf16[2,48]{1,0:T(2,128)(2,1)}, u32[]{:S(2)}) copy-start(bf16[2,48]{1,0:T(2,128)(2,1)} %param.25) | copy-start | bytes 580
  7.2 14.8 %copy-start.95 = (bf16[2,288]{1,0:T(2,128)(2,1)S(1)}, bf16[2,288]{1,0:T(2,128)(2,1)}, u32[]{:S(2)}) copy-start(bf16[2,288]{1,0:T(2,128)(2,1)} %param.17) | copy-start | bytes 3460
  7.3 14.8 %copy-start.55 = (f32[8,384]{1,0:T(8,128)S(1)}, f32[8,384]{1,0:T(8,128)}, u32[]{:S(2)}) copy-start(f32[8,384]{1,0:T(8,128)} %param.14) | copy-start | bytes 36868
  7.3 60.9 %copy-start.2 = (f32[8,256,384]{2,1,0:T(8,128)S(1)}, f32[8,256,384]{2,1,0:T(8,128)}, u32[]{:S(2)}) copy-start(f32[8,256,384]{2,1,0:T(8,128)} %param.13) | copy-start | bytes 9437188
  7.3 198.8 %all-gather.29.cloned.1.call-start = ((), (), s32[]{:S(2)}) async-start(), calls=%async_computation.20 | async-start | bytes 1990656 | tf_op jit(solution)/shard_map/all_gather | solution.py:251
  9.3 199.2 %all-gather.35.cloned.1.call-start = ((), (), s32[]{:S(2)}) async-start(), calls=%async_computation.23 | async-start | bytes 1990656 | tf_op jit(solution)/shard_map/all_gather | solution.py:251
  10.1 233.7 %all-gather.31.cloned.1.call-start = ((), (), s32[]{:S(2)}) async-start(), calls=%async_computation.21 | async-start | bytes 1327104 | tf_op jit(solution)/shard_map/all_gather | solution.py:251
  11.9 243.5 %all-gather.33.cloned.1.call-start = ((), (), s32[]{:S(2)}) async-start(), calls=%async_computation.22 | async-start | bytes 1327104 | tf_op jit(solution)/shard_map/all_gather | solution.py:251
  13.7 283.8 %all-gather.37.cloned.1.call-start = ((), (), s32[]{:S(2)}) async-start(), calls=%async_computation.24 | async-start | bytes 1327104 | tf_op jit(solution)/shard_map/all_gather | solution.py:251
  14.3 294.3 %all-gather.39.cloned.1.call-start = ((), (), s32[]{:S(2)}) async-start(), calls=%async_computation.25 | async-start | bytes 1327104 | tf_op jit(solution)/shard_map/all_gather | solution.py:251
  14.9 567.7 %reduce-scatter.21.cloned.1.call-start = ((), (), s32[]{:S(2)}) async-start(), calls=%async_computation.15 | async-start | bytes 331776 | tf_op jit(solution)/shard_map/reduce_scatter | solution.py:284
  22.1 186.4 %copy-start.44 = (bf16[8,384]{1,0:T(8,128)(2,1)}, bf16[8,384]{1,0:T(8,128)(2,1)S(1)}, u32[]{:S(2)}) copy-start(bf16[8,384]{1,0:T(8,128)(2,1)S(1)} %multiply_convert_fusion.12) | copy-start | bytes 18436
  68.5 142.5 %copy-start.46 = (f32[8,256]{1,0:T(8,128)}, f32[8,256]{1,0:T(8,128)S(1)}, u32[]{:S(2)}) copy-start(f32[8,256]{1,0:T(8,128)S(1)} %broadcast_multiply_fusion.11) | copy-start | bytes 24580
  68.5 136.9 %copy-start.80 = (bf16[1,768]{1,0:T(2,128)(2,1)S(1)}, bf16[1,768]{1,0:T(2,128)(2,1)}, u32[]{:S(2)}) copy-start(bf16[1,768]{1,0:T(2,128)(2,1)} %reshape.422) | copy-start | bytes 4612
  69.2 141.8 %copy-start.60 = (f32[8,256]{1,0:T(8,128)}, f32[8,256]{1,0:T(8,128)S(1)}, u32[]{:S(2)}) copy-start(f32[8,256]{1,0:T(8,128)S(1)} %add_rsqrt_fusion.3) | copy-start | bytes 24580
  69.9 138.7 %copy-start.57 = (f32[2304]{0:T(1024)S(1)}, f32[2304]{0:T(1024)}, u32[]{:S(2)}) copy-start(f32[2304]{0:T(1024)} %convert_element_type.361) | copy-start | bytes 27652
  134.7 103.5 %copy-start.33 = (bf16[1,384,384]{2,1,0:T(8,128)(2,1)}, bf16[1,384,384]{2,1,0:T(8,128)(2,1)S(1)}, u32[]{:S(2)}) copy-start(bf16[1,384,384]{2,1,0:T(8,128)(2,1)S(1)} %all-gather.4) | copy-start | bytes 884740
  208.5 7.4 copy-start.49
  208.5 7.4 copy-start.73
  208.5 29.7 %copy-start.42 = (f32[8,384]{1,0:T(8,128)}, f32[8,384]{1,0:T(8,128)S(1)}, u32[]{:S(2)}) copy-start(f32[8,384]{1,0:T(8,128)S(1)} %get-tuple-element.125) | copy-start | bytes 36868
  208.5 46.8 %copy-start.51 = (f32[8,384]{1,0:T(8,128)}, f32[8,384]{1,0:T(8,128)S(1)}, u32[]{:S(2)}) copy-start(f32[8,384]{1,0:T(8,128)S(1)} %get-tuple-element.120) | copy-start | bytes 36868
  211.0 53.6 %copy-start.53 = (f32[8,384]{1,0:T(8,128)}, f32[8,384]{1,0:T(8,128)S(1)}, u32[]{:S(2)}) copy-start(f32[8,384]{1,0:T(8,128)S(1)} %get-tuple-element.116) | copy-start | bytes 36868
  243.8 11.5 copy-start.5
  243.8 11.5 copy-start.85
  308.6 14.8 %copy-start.21 = (f32[8,256,384]{2,1,0:T(8,128)S(1)}, f32[8,256,384]{2,1,0:T(8,128)}, u32[]{:S(2)}) copy-start(f32[8,256,384]{2,1,0:T(8,128)} %copy-done.20) | copy-start | bytes 9437188
  308.6 14.8 %copy-start.63 = (f32[8,256]{1,0:T(8,128)S(1)}, f32[8,256]{1,0:T(8,128)}, u32[]{:S(2)}) copy-start(f32[8,256]{1,0:T(8,128)} %copy-done.62) | copy-start | bytes 24580
  308.6 14.8 %copy-start.76 = (f32[8,384]{1,0:T(8,128)S(1)}, f32[8,384]{1,0:T(8,128)}, u32[]{:S(2)}) copy-start(f32[8,384]{1,0:T(8,128)} %get-tuple-element.114) | copy-start | bytes 36868
  308.6 14.8 %copy-start.89 = (f32[8,256]{1,0:T(8,128)S(1)}, f32[8,256]{1,0:T(8,128)}, u32[]{:S(2)}) copy-start(f32[8,256]{1,0:T(8,128)} %add_rsqrt_fusion) | copy-start | bytes 24580
  308.6 14.8 %copy-start.112 = (bf16[1,384,1536]{2,1,0:T(8,128)(2,1)S(1)}, bf16[1,384,1536]{2,1,0:T(8,128)(2,1)}, u32[]{:S(2)}) copy-start(bf16[1,384,1536]{2,1,0:T(8,128)(2,1)} %all-gather.37.cloned.1.call-done) | copy-start | bytes 3538948
  347.1 9.6 copy-start.11
  347.1 9.6 copy-start.17
  415.3 7.3 copy-start.25
  415.3 7.3 copy-start.31
  415.3 7.3 copy-start.52
  425.3 18.4 %copy-start.22 = (f32[8,256,384]{2,1,0:T(8,128)}, f32[8,256,384]{2,1,0:T(8,128)S(1)}, u32[]{:S(2)}) copy-start(f32[8,256,384]{2,1,0:T(8,128)S(1)} %get-tuple-element.85) | copy-start | bytes 9437188
  425.3 13.9 %copy-start.109 = (bf16[1,384,1536]{2,1,0:T(8,128)(2,1)S(1)}, bf16[1,384,1536]{2,1,0:T(8,128)(2,1)}, u32[]{:S(2)}) copy-start(bf16[1,384,1536]{2,1,0:T(8,128)(2,1)} %all-gather.31.cloned.1.call-done) | copy-start | bytes 3538948
  451.8 9.3 copy-start.16
  467.4 22.8 %copy-start.29 = (bf16[8,256,384]{1,2,0:T(8,128)(2,1)S(1)}, bf16[8,256,384]{1,2,0:T(8,128)(2,1)}, u32[]{:S(2)}) copy-start(bf16[8,256,384]{1,2,0:T(8,128)(2,1)} %copy.130) | copy-start | bytes 4718596
  490.2 22.9 %copy-start.15 = (bf16[8,6,64,256]{3,2,1,0:T(8,128)(2,1)S(1)}, bf16[8,6,64,256]{3,2,1,0:T(8,128)(2,1)}, u32[]{:S(2)}) copy-start(bf16[8,6,64,256]{3,2,1,0:T(8,128)(2,1)} %copy-done.14) | copy-start | bytes 4718596
  516.2 119.9 %reduce-scatter.19.cloned.1.call-start = ((), (), s32[]{:S(2)}) async-start(), calls=%async_computation.14 | async-start | bytes 331776 | tf_op jit(solution)/shard_map/reduce_scatter | solution.py:284
  521.5 8.2 copy-start.47
  521.5 8.2 copy-start.50
  521.5 8.2 copy-start.61
  539.1 97.0 %copy-start.79 = (f32[8,384]{1,0:T(8,128)S(1)}, f32[8,384]{1,0:T(8,128)}, u32[]{:S(2)}) copy-start(f32[8,384]{1,0:T(8,128)} %get-tuple-element.115) | copy-start | bytes 36868
  543.0 156.3 %all-reduce.29.cloned.1.call-start = ((), (), s32[]{:S(2)}) async-start(), calls=%async_computation.26 | async-start | bytes 174080
  579.3 56.8 %copy-start.68 = (bf16[1152]{0:T(1024)(128)(2,1)}, bf16[1152]{0:T(1024)(128)(2,1)S(1)}, u32[]{:S(2)}) copy-start(bf16[1152]{0:T(1024)(128)(2,1)S(1)} %dynamic-update-slice.10) | copy-start | bytes 6916
  579.5 56.6 %copy-start.67 = (bf16[1152]{0:T(1024)(128)(2,1)}, bf16[1152]{0:T(1024)(128)(2,1)S(1)}, u32[]{:S(2)}) copy-start(bf16[1152]{0:T(1024)(128)(2,1)S(1)} %dynamic-update-slice.11) | copy-start | bytes 6916
  636.1 102.2 %reduce-scatter.17.cloned.1.call-start = ((), (), s32[]{:S(2)}) async-start(), calls=%async_computation.13 | async-start | bytes 995328 | tf_op jit(solution)/shard_map/reduce_scatter | solution.py:278
  642.9 159.8 %reduce-scatter.15.cloned.1.call-start = ((), (), s32[]{:S(2)}) async-start(), calls=%async_computation.12 | async-start | bytes 995328 | tf_op jit(solution)/shard_map/reduce_scatter | solution.py:278
  649.4 7.7 copy-start.72
  649.4 220.1 %reduce-scatter.25.cloned.1.call-start = ((), (), s32[]{:S(2)}) async-start(), calls=%async_computation.17 | async-start | bytes 1327104 | tf_op jit(solution)/shard_map/reduce_scatter | solution.py:290
  657.1 279.5 %reduce-scatter.29.cloned.1.call-start = ((), (), s32[]{:S(2)}) async-start(), calls=%async_computation.19 | async-start | bytes 1327104 | tf_op jit(solution)/shard_map/reduce_scatter | solution.py:296
  665.4 8.4 copy-start.70
  665.4 338.2 %reduce-scatter.27.cloned.1.call-start = ((), (), s32[]{:S(2)}) async-start(), calls=%async_computation.18 | async-start | bytes 1327104 | tf_op jit(solution)/shard_map/reduce_scatter | solution.py:296
  673.7 8.0 copy-start.45
  673.7 396.8 %reduce-scatter.23.cloned.1.call-start = ((), (), s32[]{:S(2)}) async-start(), calls=%async_computation.16 | async-start | bytes 1327104 | tf_op jit(solution)/shard_map/reduce_scatter | solution.py:290
  681.4 458.5 %reduce-scatter.13.cloned.1.call-start = ((), (), s32[]{:S(2)}) async-start(), calls=%async_computation.11 | async-start | bytes 1990656 | tf_op jit(solution)/shard_map/reduce_scatter | solution.py:272
  684.5 524.1 %reduce-scatter.11.cloned.1.call-start = ((), (), s32[]{:S(2)}) async-start(), calls=%async_computation.10 | async-start | bytes 1990656 | tf_op jit(solution)/shard_map/reduce_scatter | solution.py:272
  687.4 561.9 %all-reduce.31.cloned.1.call-start = ((), (), s32[]{:S(2)}) async-start(), calls=%async_computation.27 | async-start | bytes 2506752 | tf_op jit(solution)/shard_map/psum | solution.py:308
  (70 other events, 293.9 us)
Sparse Core Ops, SparseCore 0:
  10.8 48.9 all-gather.28
  62.6 47.1 all-gather.34
  112.6 45.6 all-gather.30
  160.3 44.6 all-gather.32
  207.6 39.5 all-gather.36
  249.3 39.7 all-gather.38
  516.3 57.1 reduce-scatter.20
  577.4 58.6 reduce-scatter.18
  640.5 31.1 all-reduce.28
  675.4 62.8 reduce-scatter.16
  741.7 60.9 reduce-scatter.14
  806.0 63.4 reduce-scatter.24
  872.9 63.6 reduce-scatter.28
  939.8 63.7 reduce-scatter.26
  1006.8 63.6 reduce-scatter.22
  1073.8 65.9 reduce-scatter.12
  1143.1 65.4 reduce-scatter.10
  1211.4 37.8 all-reduce.30
